TPU v7x, 256 devices: a whole 4x4x8 slice. The times are simulated.
256 devices in a mesh: wide: 16 (over y, z_hi), narrow: 16 (over x, z_lo, core).
Axes of the slice: x: 4, y: 4, z: 8 (z_hi: 4, z_lo: 2; z = z_hi * 2 + z_lo), core: 2. Of those that a mesh axis runs over, the one named last changes fastest.
Arguments:
- features: bfloat16 [65536, 768], P(('wide', 'narrow'))
- proj_weight: bfloat16 [768, 512], replicated, may hold values from -0.21875 to 0.21875
- bias: float32 [512], replicated, may hold values from -1.5 to 1.5
- disc_weight: float32 [512, 512], replicated, may hold values from -0.25 to 0.25
- adjacency: int32 [16, 16, 24, 256, 256], P('wide', 'narrow'), may hold values from 0 to 3
- row_block: int32 [16, 16, 24], P('wide', 'narrow'), may hold values from 0 to 15
- col_block: int32 [16, 16, 24], P('wide', 'narrow'), may hold values from 0 to 15
- block_count: int32 [16, 16], P('wide', 'narrow'), may hold values from 1 to 24, as said below
- degree: int32 [65536], replicated, may hold values from 6 to 65
- corrupt_source: int32 [256], replicated, may hold values from 0 to 255, as said below
Outputs:
- hidden: bfloat16 [65536, 512], P(('wide', 'narrow'))
- scores: float32 [2, 65536], P(None, ('wide', 'narrow'))
- loss: float32 [], replicated
Inputs may be any that keep to these rules, and one draw needn't show every extreme that they name: Only slots below block_count of a tile take part; some tile holds 24 live slots in every draw. corrupt_source is a permutation of the blocks, and block g and block corrupt_source[g] have equal g % 16.
All inputs are finite; a program needn't handle non-finite values.
Results may differ from a plain program's by a relative error of at most 0.0056.
Values may be sent and summed in bfloat16 or wider, within the bound.
No kernel may reach another device: no remote copies, remote signals or barrier semaphores. Data moves between devices by JAX's collectives and lax.ppermute only.
A program may use at most 128 MiB of HBM per device.

v0:
```python
import jax
import jax.numpy as jnp
from jax import lax
from jax.sharding import PartitionSpec as P


def shards(
    features,
    proj_weight,
    bias,
    disc_weight,
    adjacency,
    row_block,
    col_block,
    block_count,
    degree,
    corrupt_source,
):
    rows_dev = features.shape[0]
    block_len = adjacency.shape[-1]
    blocks_dev = rows_dev // block_len
    hidden_width = proj_weight.shape[1]
    wide_size = lax.axis_size("wide")
    narrow_size = lax.axis_size("narrow")
    wide_at = lax.axis_index("wide")
    narrow_at = lax.axis_index("narrow")
    tile_height = blocks_dev * narrow_size
    tile_width = blocks_dev * wide_size
    panel = jnp.dot(
        lax.all_gather(features, "wide", axis=0, tiled=True),
        proj_weight,
        preferred_element_type=jnp.float32,
    ).astype(jnp.bfloat16)
    clean_blocks = panel.reshape(tile_width, block_len, hidden_width)
    local_cols = jnp.arange(tile_width, dtype=jnp.int32)
    global_cols = (
        local_cols // blocks_dev * narrow_size + narrow_at
    ) * blocks_dev + local_cols % blocks_dev
    sources = jnp.take(corrupt_source, global_cols)
    source_local = sources // blocks_dev // narrow_size * blocks_dev + sources % blocks_dev
    corrupt_blocks = jnp.take(clean_blocks, source_local, axis=0)
    inv_root = lax.rsqrt(degree.astype(jnp.float32))
    col_roots = lax.dynamic_index_in_dim(
        inv_root.reshape(wide_size, narrow_size, rows_dev), narrow_at, 1, keepdims=False
    )
    row_roots = lax.dynamic_index_in_dim(
        inv_root.reshape(wide_size, tile_height, block_len), wide_at, 0, keepdims=False
    )
    slot_rows = row_block[0, 0]
    slot_cols = col_block[0, 0]
    normed = (
        adjacency[0, 0].astype(jnp.float32)
        * row_roots[slot_rows][:, :, None]
        * col_roots[slot_cols][:, None, :]
    ).astype(jnp.bfloat16)
    live_slots = block_count[0, 0]
    joined = jnp.concatenate((clean_blocks, corrupt_blocks), axis=2)
    width = joined.shape[2]

    def add_slot(slot, totals):
        term = jnp.dot(normed[slot], joined[slot_cols[slot]], preferred_element_type=jnp.float32)
        return totals.at[slot_rows[slot]].add(term)

    totals = lax.fori_loop(
        jnp.int32(0), live_slots, add_slot, jnp.zeros((tile_height, block_len, width), jnp.float32)
    )
    summed = lax.psum_scatter(
        totals.reshape(tile_height * block_len, width), "narrow", scatter_dimension=0, tiled=True
    )
    clean_sum = summed[:, :hidden_width]
    corrupt_sum = summed[:, hidden_width:]
    own_clean = lax.dynamic_slice_in_dim(clean_blocks, wide_at * blocks_dev, blocks_dev, 0).reshape(
        rows_dev, hidden_width
    )
    own_corrupt = lax.dynamic_slice_in_dim(
        corrupt_blocks, wide_at * blocks_dev, blocks_dev, 0
    ).reshape(rows_dev, hidden_width)
    own_degree = lax.dynamic_index_in_dim(
        degree.reshape(wide_size * narrow_size, rows_dev),
        wide_at * narrow_size + narrow_at,
        0,
        keepdims=False,
    )
    degree_float = own_degree.astype(jnp.float32)[:, None]
    clean_h = jnp.maximum(clean_sum + own_clean.astype(jnp.float32) / degree_float + bias, 0.0)
    corrupt_h = jnp.maximum(
        corrupt_sum + own_corrupt.astype(jnp.float32) / degree_float + bias, 0.0
    )
    node_total = rows_dev * wide_size * narrow_size
    column_total = lax.psum(jnp.sum(clean_h, axis=0), ("wide", "narrow"))
    summary = jax.nn.sigmoid(column_total / node_total)
    probe = jnp.dot(disc_weight, summary, precision=lax.Precision.HIGHEST)
    clean_score = jnp.dot(clean_h, probe, precision=lax.Precision.HIGHEST)
    corrupt_score = jnp.dot(corrupt_h, probe, precision=lax.Precision.HIGHEST)
    local_terms = jnp.sum(jax.nn.softplus(-clean_score)) + jnp.sum(jax.nn.softplus(corrupt_score))
    loss = lax.psum(local_terms, ("wide", "narrow")) / (2 * node_total)
    return (clean_h.astype(jnp.bfloat16), jnp.stack((clean_score, corrupt_score)), loss)


def solution(mesh):
    placed = (
        P(("wide", "narrow"), None),
        P(),
        P(),
        P(),
        P("wide", "narrow", None, None, None),
        P("wide", "narrow", None),
        P("wide", "narrow", None),
        P("wide", "narrow"),
        P(),
        P(),
    )
    return jax.shard_map(
        shards,
        mesh=mesh,
        in_specs=placed,
        out_specs=(P(("wide", "narrow"), None), P(None, ("wide", "narrow")), P()),
        check_vma=False,
    )
```

profile of v0, /device:TPU:1, one launch (start us, length us, event | category | flops | bytes accessed | tf_op | source)
XLA Modules:
  0.0 729.2 jit_solution(8691298326891454932)
XLA Ops:
  12.4 4.5 fusion.7
  16.9 88.1 %all-gather.2.cloned.1.call-done = bf16[4096,768]{1,0:T(8,128)(2,1)} async-done(((bf16[256,768]{1,0:T(8,128)(2,1)}), bf16[4096,768]{1,0:T(8,128)(2,1)}) %all-gather.2.cloned.1.call-update) | async-done | bytes 6291472 | tf_op jit(solution)/shard_map/all_gather | solution.py:30
  105.0 7.8 %convolution_convert_fusion = bf16[4096,512]{1,0:T(8,128)(2,1)} fusion(bf16[4096,768]{1,0:T(8,128)(2,1)} %all-gather.2.cloned.1.call-done, bf16[768,512]{1,0:T(8,128)(2,1)S(1)} %copy-done.6), kind=kOutput, calls=%fused_computation.17 | convolution fusion | flops 3223322624 | bytes 11272192 | tf_op jit(solution)/shard_map/dot_general | solution.py:29
  112.8 4.9 gather_fusion.3
  117.8 4.6 broadcast_select_fusion
  122.4 7.9 %pad_maximum_fusion = bf16[16,256,1024]{2,1,0:T(8,128)(2,1)} fusion(bf16[16,256,512]{2,1,0:T(8,128)(2,1)} %broadcast_select_fusion, bf16[16,256,512]{2,1,0:T(8,128)(2,1)} %bitcast.86), kind=kLoop, calls=%fused_computation.13 | loop fusion | flops 16777216 | bytes 16777216 | tf_op jit(solution)/shard_map/concatenate | solution.py:57
  130.3 7.9 %broadcast_in_dim.15 = f32[16,256,1024]{2,1,0:T(8,128)} broadcast(f32[]{:T(128)} %constant.146.clone.1), dimensions={} | broadcast | bytes 16777220 | tf_op jit(solution)/shard_map/broadcast_in_dim | solution.py:65
  138.2 236.4 %while.11 = (s32[]{:T(128)}, f32[16,256,1024]{2,1,0:T(8,128)}, s32[]{:T(128)}, s32[24]{0:T(128)S(1)}, bf16[24,256,256]{2,1,0:T(8,128)(2,1)}, /*index=5*/s32[24]{...) while((s32[]{:T(128)}, f32[16,256,1024]{2,1,0:T(8,128)}, ...), condition=%wide.region_2.3_spmd, body=%wide.region_0.2_spmd.sunk | while | flops 134742048 | bytes 2753824 | solution.py:64
  144.6 3.4 fusion.43
  154.4 3.4 fusion.43
  164.3 3.5 fusion.43
  174.2 3.4 fusion.43
  184.0 3.4 fusion.43
  193.8 3.4 fusion.43
  203.6 3.4 fusion.43
  213.5 3.4 fusion.43
  223.3 3.4 fusion.43
  233.1 3.4 fusion.43
  243.0 3.4 fusion.43
  252.8 3.4 fusion.43
  262.6 3.4 fusion.43
  282.2 3.4 fusion.43
  292.1 3.4 fusion.43
  301.9 3.4 fusion.43
  321.5 3.4 fusion.43
  331.3 3.4 fusion.43
  341.1 3.4 fusion.43
  360.7 3.4 fusion.43
  370.6 3.4 fusion.43
  375.6 186.8 %reduce-scatter.2.cloned.1.call-done = f32[256,1024]{1,0:T(8,128)} async-done(((f32[4096,1024]{1,0:T(8,128)}), f32[256,1024]{1,0:T(8,128)}) %reduce-scatter.2.cloned.1.call-update) | async-done | bytes 1048592 | tf_op jit(solution)/shard_map/reduce_scatter | solution.py:67
  563.7 77.1 %psum.14 = f32[512]{0:T(512)S(1)} all-reduce(f32[512]{0:T(512)S(1)} %get-tuple-element.68), channel_id=1, replica_groups=mesh['wide'=16,'narrow'=16] {'wide','narrow'}, use_global_device_ids=true, to_apply=%region_5.6 | all-reduce | flops 512 | bytes 4096 | tf_op jit(solution)/shard_map/psum | solution.py:90
  648.0 72.6 %psum.15 = f32[]{:T(128)} all-reduce(f32[]{:T(128)S(6)} %add.223), channel_id=1, replica_groups=mesh['wide'=16,'narrow'=16] {'wide','narrow'}, use_global_device_ids=true, to_apply=%region_8.9 | all-reduce | flops 1 | bytes 8 | tf_op jit(solution)/shard_map/psum | solution.py:96
  (120 shorter events, 68.7 us)
Async XLA Ops:
  7.2 633.7 %copy-start = (f32[512,512]{1,0:T(8,128)S(1)}, f32[512,512]{1,0:T(8,128)}, u32[]{:S(2)}) copy-start(f32[512,512]{1,0:T(8,128)} %param.17) | copy-start | bytes 3145732
  7.2 97.8 %copy-start.6 = (bf16[768,512]{1,0:T(8,128)(2,1)S(1)}, bf16[768,512]{1,0:T(8,128)(2,1)}, u32[]{:S(2)}) copy-start(bf16[768,512]{1,0:T(8,128)(2,1)} %param.15) | copy-start | bytes 2359300
  7.2 97.8 %all-gather.2.cloned.1.call-start = ((), (), s32[]{:S(2)}) async-start(), calls=%async_computation.1 | async-start | bytes 6684672 | tf_op jit(solution)/shard_map/all_gather | solution.py:30
  7.9 554.5 %reduce-scatter.2.cloned.1.call-start = ((), (), s32[]{:S(2)}) async-start(), calls=%async_computation.2 | async-start | bytes 17825792 | tf_op jit(solution)/shard_map/reduce_scatter | solution.py:67
  130.3 7.9 %copy-start.2 = (s32[3]{0:T(128)S(1)}, s32[3]{0:T(128)}, u32[]{:S(2)}) copy-start(s32[3]{0:T(128)} %constant.143.clone.1) | copy-start | bytes 40
  130.3 7.9 %copy-start.4 = (s32[1,1,24]{2,1,0:T(1,128)S(1)}, s32[1,1,24]{2,1,0:T(1,128)}, u32[]{:S(2)}) copy-start(s32[1,1,24]{2,1,0:T(1,128)} %param.19) | copy-start | bytes 292
  130.3 7.9 %copy-start.5 = (s32[1,1,24]{2,1,0:T(1,128)S(1)}, s32[1,1,24]{2,1,0:T(1,128)}, u32[]{:S(2)}) copy-start(s32[1,1,24]{2,1,0:T(1,128)} %param.20) | copy-start | bytes 292
  374.6 1.0 copy-start.1
  374.6 187.8 %copy-start.3 = (f32[512]{0:T(512)S(1)}, f32[512]{0:T(512)}, u32[]{:S(2)}) copy-start(f32[512]{0:T(512)} %param.16) | copy-start | bytes 6148
Sparse Core Ops, SparseCore 0:
  10.5 94.4 all-gather.1
  374.7 187.6 reduce-scatter.1
where the time goes:
time: 732 us; the launch traced here: 729 us
  waiting for transfers between devices  276 us (38%)
  blocking collectives  150 us (20%)
  loops' own time  110 us (15%)
  matrix products  92.1 us (13%)
  local copies, waits for them, and re-layouts  44.7 us (6%)
  other arithmetic  39.8 us (5%)
  between operations  17.3 us (2%)
    reduce_scatter x1, waiting for transfers between devices, shards(): lax.psum_scatter(totals.reshape(tile_height * block_len, width), 'narrow'...  187 us
    another operation x1, loops' own time, shards(): lax.fori_loop(jnp.int32(0), live_slots, add_slot, jnp.zeros((tile_height,...  110 us
    all_gather x1, waiting for transfers between devices, shards(): lax.all_gather(features, 'wide', axis=0, tiled=True)  88.1 us
    dot_general x24, matrix products, add_slot(): jnp.dot(normed[slot], joined[slot_cols[slot]], preferred_element_type=jnp...  81.1 us
    psum x1, blocking collectives, shards(): column_total = lax.psum(jnp.sum(clean_h, axis=0), ('wide', 'narrow'))  77.1 us
    psum x1, blocking collectives, shards(): loss = lax.psum(local_terms, ('wide', 'narrow')) / (2 * node_total)  72.6 us
    another operation x24, other arithmetic  17.1 us
  transfers between devices with their start and end apart: 2, of which 2 were waited for; matrix products, arithmetic and copies ran while one was open for 1% of the time, Pallas kernels for 0%

commit v1 on v0

--- a/solution.py
+++ b/solution.py
@@ -87,7 +87,7 @@
         corrupt_sum + own_corrupt.astype(jnp.float32) / degree_float + bias, 0.0
     )
     node_total = rows_dev * wide_size * narrow_size
-    column_total = lax.psum(jnp.sum(clean_h, axis=0), ("wide", "narrow"))
+    column_total = lax.psum(lax.psum(jnp.sum(clean_h, axis=0), "narrow"), "wide")
     summary = jax.nn.sigmoid(column_total / node_total)
     probe = jnp.dot(disc_weight, summary, precision=lax.Precision.HIGHEST)
     clean_score = jnp.dot(clean_h, probe, precision=lax.Precision.HIGHEST)

time: 732 us -> 728 us (level)
    psum x1 -> x2, blocking collectives: 77.1 us -> 65.9 us  [the longest x1 37.2 us: shards(): lax.psum(lax.psum(jnp.sum(clean_h, axis=0), 'narrow'), 'wide')]
where the time goes in v1:
time: 728 us; the launch traced here: 725 us
  waiting for transfers between devices  276 us (38%)
  blocking collectives  145 us (20%)
  loops' own time  110 us (15%)
  matrix products  92.1 us (13%)
  local copies, waits for them, and re-layouts  44.7 us (6%)
  other arithmetic  39.8 us (5%)
  between operations  17.3 us (2%)
    reduce_scatter x1, waiting for transfers between devices, shards(): lax.psum_scatter(totals.reshape(tile_height * block_len, width), 'narrow'...  187 us
    another operation x1, loops' own time, shards(): lax.fori_loop(jnp.int32(0), live_slots, add_slot, jnp.zeros((tile_height,...  110 us
    all_gather x1, waiting for transfers between devices, shards(): lax.all_gather(features, 'wide', axis=0, tiled=True)  88.1 us
    dot_general x24, matrix products, add_slot(): jnp.dot(normed[slot], joined[slot_cols[slot]], preferred_element_type=jnp...  81.1 us
    psum x1, blocking collectives, shards(): loss = lax.psum(local_terms, ('wide', 'narrow')) / (2 * node_total)  79.3 us
    psum x1, blocking collectives, shards(): lax.psum(lax.psum(jnp.sum(clean_h, axis=0), 'narrow'), 'wide')  37.2 us
    psum x1, blocking collectives, shards(): lax.psum(jnp.sum(clean_h, axis=0), 'narrow')  28.7 us
    another operation x24, other arithmetic  17.1 us
  transfers between devices with their start and end apart: 2, of which 2 were waited for; matrix products, arithmetic and copies ran while one was open for 1% of the time, Pallas kernels for 0%

profile of v1, /device:TPU:1, one launch (start us, length us, event | category | flops | bytes accessed | tf_op | source)
XLA Modules:
  0.0 724.7 jit_solution(17921881761844932424)
XLA Ops:
  12.4 4.5 fusion.7
  16.9 88.1 %all-gather.2.cloned.1.call-done = bf16[4096,768]{1,0:T(8,128)(2,1)} async-done(((bf16[256,768]{1,0:T(8,128)(2,1)}), bf16[4096,768]{1,0:T(8,128)(2,1)}) %all-gather.2.cloned.1.call-update) | async-done | bytes 6291472 | tf_op jit(solution)/shard_map/all_gather | solution.py:30
  105.0 7.8 %convolution_convert_fusion = bf16[4096,512]{1,0:T(8,128)(2,1)} fusion(bf16[4096,768]{1,0:T(8,128)(2,1)} %all-gather.2.cloned.1.call-done, bf16[768,512]{1,0:T(8,128)(2,1)S(1)} %copy-done.6), kind=kOutput, calls=%fused_computation.17 | convolution fusion | flops 3223322624 | bytes 11272192 | tf_op jit(solution)/shard_map/dot_general | solution.py:29
  112.8 4.9 gather_fusion.3
  117.8 4.6 broadcast_select_fusion
  122.4 7.9 %pad_maximum_fusion = bf16[16,256,1024]{2,1,0:T(8,128)(2,1)} fusion(bf16[16,256,512]{2,1,0:T(8,128)(2,1)} %broadcast_select_fusion, bf16[16,256,512]{2,1,0:T(8,128)(2,1)} %bitcast.86), kind=kLoop, calls=%fused_computation.13 | loop fusion | flops 16777216 | bytes 16777216 | tf_op jit(solution)/shard_map/concatenate | solution.py:57
  130.3 7.9 %broadcast_in_dim.15 = f32[16,256,1024]{2,1,0:T(8,128)} broadcast(f32[]{:T(128)} %constant.146.clone.1), dimensions={} | broadcast | bytes 16777220 | tf_op jit(solution)/shard_map/broadcast_in_dim | solution.py:65
  138.2 236.4 %while.11 = (s32[]{:T(128)}, f32[16,256,1024]{2,1,0:T(8,128)}, s32[]{:T(128)}, s32[24]{0:T(128)S(1)}, bf16[24,256,256]{2,1,0:T(8,128)(2,1)}, /*index=5*/s32[24]{...) while((s32[]{:T(128)}, f32[16,256,1024]{2,1,0:T(8,128)}, ...), condition=%wide.region_2.3_spmd, body=%wide.region_0.2_spmd.sunk | while | flops 134742048 | bytes 2753824 | solution.py:64
  144.6 3.4 fusion.43
  154.4 3.4 fusion.43
  164.3 3.5 fusion.43
  174.2 3.4 fusion.43
  184.0 3.4 fusion.43
  193.8 3.4 fusion.43
  203.6 3.4 fusion.43
  213.5 3.4 fusion.43
  223.3 3.4 fusion.43
  233.1 3.4 fusion.43
  243.0 3.4 fusion.43
  252.8 3.4 fusion.43
  262.6 3.4 fusion.43
  282.2 3.4 fusion.43
  292.1 3.4 fusion.43
  301.9 3.4 fusion.43
  321.5 3.4 fusion.43
  331.3 3.4 fusion.43
  360.7 3.4 fusion.43
  370.6 3.4 fusion.43
  375.6 186.8 %reduce-scatter.2.cloned.1.call-done = f32[256,1024]{1,0:T(8,128)} async-done(((f32[4096,1024]{1,0:T(8,128)}), f32[256,1024]{1,0:T(8,128)}) %reduce-scatter.2.cloned.1.call-update) | async-done | bytes 1048592 | tf_op jit(solution)/shard_map/reduce_scatter | solution.py:67
  563.7 28.7 %psum.21 = f32[512]{0:T(512)S(1)} all-reduce(f32[512]{0:T(512)S(1)} %get-tuple-element.68), channel_id=1, replica_groups=mesh['wide'=16,'narrow'=16] {'narrow'}, use_global_device_ids=true, to_apply=%region_5.6 | all-reduce | flops 512 | bytes 4096 | tf_op jit(solution)/shard_map/psum | solution.py:90
  592.4 37.2 %psum.22 = f32[512]{0:T(512)S(1)} all-reduce(f32[512]{0:T(512)S(1)} %psum.21), channel_id=1, replica_groups=mesh['wide'=16,'narrow'=16] {'wide'}, use_global_device_ids=true, to_apply=%region_6.7 | all-reduce | flops 512 | bytes 4096 | tf_op jit(solution)/shard_map/psum | solution.py:90
  636.8 79.3 %psum.23 = f32[]{:T(128)} all-reduce(f32[]{:T(128)S(6)} %add.225), channel_id=1, replica_groups=mesh['wide'=16,'narrow'=16] {'wide','narrow'}, use_global_device_ids=true, to_apply=%region_9.10 | all-reduce | flops 1 | bytes 8 | tf_op jit(solution)/shard_map/psum | solution.py:96
  (121 shorter events, 72.0 us)
Async XLA Ops:
  7.2 622.5 %copy-start = (f32[512,512]{1,0:T(8,128)S(1)}, f32[512,512]{1,0:T(8,128)}, u32[]{:S(2)}) copy-start(f32[512,512]{1,0:T(8,128)} %param.17) | copy-start | bytes 3145732
  7.2 97.8 %copy-start.6 = (bf16[768,512]{1,0:T(8,128)(2,1)S(1)}, bf16[768,512]{1,0:T(8,128)(2,1)}, u32[]{:S(2)}) copy-start(bf16[768,512]{1,0:T(8,128)(2,1)} %param.15) | copy-start | bytes 2359300
  7.2 97.8 %all-gather.2.cloned.1.call-start = ((), (), s32[]{:S(2)}) async-start(), calls=%async_computation.1 | async-start | bytes 6684672 | tf_op jit(solution)/shard_map/all_gather | solution.py:30
  7.9 554.5 %reduce-scatter.2.cloned.1.call-start = ((), (), s32[]{:S(2)}) async-start(), calls=%async_computation.2 | async-start | bytes 17825792 | tf_op jit(solution)/shard_map/reduce_scatter | solution.py:67
  130.3 7.9 %copy-start.2 = (s32[3]{0:T(128)S(1)}, s32[3]{0:T(128)}, u32[]{:S(2)}) copy-start(s32[3]{0:T(128)} %constant.143.clone.1) | copy-start | bytes 40
  130.3 7.9 %copy-start.4 = (s32[1,1,24]{2,1,0:T(1,128)S(1)}, s32[1,1,24]{2,1,0:T(1,128)}, u32[]{:S(2)}) copy-start(s32[1,1,24]{2,1,0:T(1,128)} %param.19) | copy-start | bytes 292
  130.3 7.9 %copy-start.5 = (s32[1,1,24]{2,1,0:T(1,128)S(1)}, s32[1,1,24]{2,1,0:T(1,128)}, u32[]{:S(2)}) copy-start(s32[1,1,24]{2,1,0:T(1,128)} %param.20) | copy-start | bytes 292
  374.6 1.0 copy-start.1
  374.6 187.8 %copy-start.3 = (f32[512]{0:T(512)S(1)}, f32[512]{0:T(512)}, u32[]{:S(2)}) copy-start(f32[512]{0:T(512)} %param.16) | copy-start | bytes 6148
Sparse Core Ops, SparseCore 0:
  10.5 94.4 all-gather.1
  374.7 187.6 reduce-scatter.1

commit v2 on v0

--- a/solution.py
+++ b/solution.py
@@ -87,7 +87,7 @@
         corrupt_sum + own_corrupt.astype(jnp.float32) / degree_float + bias, 0.0
     )
     node_total = rows_dev * wide_size * narrow_size
-    column_total = lax.psum(jnp.sum(clean_h, axis=0), ("wide", "narrow"))
+    column_total = jnp.sum(lax.all_gather(jnp.sum(clean_h, axis=0), ("wide", "narrow")), axis=0)
     summary = jax.nn.sigmoid(column_total / node_total)
     probe = jnp.dot(disc_weight, summary, precision=lax.Precision.HIGHEST)
     clean_score = jnp.dot(clean_h, probe, precision=lax.Precision.HIGHEST)

time: 732 us -> 1000 us (1.37)
  blocking collectives: 150 us -> 420 us
    all_gather x0 -> x1, blocking collectives: none -> 348 us  [shards(): lax.all_gather(jnp.sum(clean_h, axis=0), ('wide', 'narrow'))]
    psum x1 -> x0, blocking collectives: 77.1 us -> none  [shards(): column_total = lax.psum(jnp.sum(clean_h, axis=0), ('wide', 'narrow'))]
where the time goes in v2:
time: 1000 us
  blocking collectives  420 us (42%)
  waiting for transfers between devices  276 us (28%)
  loops' own time  110 us (11%)
  matrix products  92.1 us (9%)
  local copies, waits for them, and re-layouts  44.7 us (4%)
  other arithmetic  40.1 us (4%)
  between operations  17.3 us (2%)
    all_gather x1, blocking collectives, shards(): lax.all_gather(jnp.sum(clean_h, axis=0), ('wide', 'narrow'))  348 us
    reduce_scatter x1, waiting for transfers between devices, shards(): lax.psum_scatter(totals.reshape(tile_height * block_len, width), 'narrow'...  187 us
    another operation x1, loops' own time, shards(): lax.fori_loop(jnp.int32(0), live_slots, add_slot, jnp.zeros((tile_height,...  110 us
    all_gather x1, waiting for transfers between devices, shards(): lax.all_gather(features, 'wide', axis=0, tiled=True)  88.1 us
    dot_general x24, matrix products, add_slot(): jnp.dot(normed[slot], joined[slot_cols[slot]], preferred_element_type=jnp...  81.1 us
    psum x1, blocking collectives, shards(): loss = lax.psum(local_terms, ('wide', 'narrow')) / (2 * node_total)  72.6 us
  transfers between devices with their start and end apart: 2, of which 2 were waited for; matrix products, arithmetic and copies ran while one was open for 1% of the time, Pallas kernels for 0%

profile of v2, /device:TPU:1, one launch (start us, length us, event | category | flops | bytes accessed | tf_op | source)
XLA Modules:
  0.0 999.9 jit_solution(1237543420022804788)
XLA Ops:
  12.4 4.5 fusion.7
  16.9 88.1 %all-gather.4.cloned.1.call-done = bf16[4096,768]{1,0:T(8,128)(2,1)} async-done(((bf16[256,768]{1,0:T(8,128)(2,1)}), bf16[4096,768]{1,0:T(8,128)(2,1)}) %all-gather.4.cloned.1.call-update) | async-done | bytes 6291472 | tf_op jit(solution)/shard_map/all_gather | solution.py:30
  105.0 7.8 convolution_convert_fusion
  112.8 4.9 gather_fusion.3
  117.8 4.6 broadcast_select_fusion
  122.4 7.9 pad_maximum_fusion
  130.3 7.9 broadcast_in_dim.15
  138.2 236.4 %while.11 = (s32[]{:T(128)}, f32[16,256,1024]{2,1,0:T(8,128)}, s32[]{:T(128)}, s32[24]{0:T(128)S(1)}, bf16[24,256,256]{2,1,0:T(8,128)(2,1)}, /*index=5*/s32[24]{...) while((s32[]{:T(128)}, f32[16,256,1024]{2,1,0:T(8,128)}, ...), condition=%wide.region_2.3_spmd, body=%wide.region_0.2_spmd.sunk | while | flops 134742048 | bytes 2753824 | solution.py:64
  144.6 3.4 fusion.43
  154.4 3.4 fusion.43
  164.3 3.5 fusion.43
  174.2 3.4 fusion.43
  184.0 3.4 fusion.43
  193.8 3.4 fusion.43
  203.6 3.4 fusion.43
  213.5 3.4 fusion.43
  223.3 3.4 fusion.43
  233.1 3.4 fusion.43
  243.0 3.4 fusion.43
  252.8 3.4 fusion.43
  262.6 3.4 fusion.43
  282.2 3.4 fusion.43
  292.1 3.4 fusion.43
  301.9 3.4 fusion.43
  321.5 3.4 fusion.43
  331.3 3.4 fusion.43
  341.1 3.4 fusion.43
  360.7 3.4 fusion.43
  370.6 3.4 fusion.43
  375.6 186.8 %reduce-scatter.2.cloned.1.call-done = f32[256,1024]{1,0:T(8,128)} async-done(((f32[4096,1024]{1,0:T(8,128)}), f32[256,1024]{1,0:T(8,128)}) %reduce-scatter.2.cloned.1.call-update) | async-done | bytes 1048592 | tf_op jit(solution)/shard_map/reduce_scatter | solution.py:67
  563.7 347.5 %all-gather.1 = f32[256,1,512]{2,1,0:T(1,128)S(1)} all-gather(f32[1,1,512]{2,1,0:T(1,128)S(1)} %bitcast.90), channel_id=2, replica_groups=mesh['wide'=16,'narrow'=16] {'wide','narrow'}, dimensions={0}, use_global_device_ids=true | all-gather | bytes 526336 | tf_op jit(solution)/shard_map/all_gather | solution.py:90
  918.7 72.6 %psum.7 = f32[]{:T(128)} all-reduce(f32[]{:T(128)S(6)} %add.221), channel_id=1, replica_groups=mesh['wide'=16,'narrow'=16] {'wide','narrow'}, use_global_device_ids=true, to_apply=%region_8.9 | all-reduce | flops 1 | bytes 8 | tf_op jit(solution)/shard_map/psum | solution.py:96
  (121 shorter events, 69.0 us)
Async XLA Ops:
  7.2 904.4 %copy-start = (f32[512,512]{1,0:T(8,128)S(1)}, f32[512,512]{1,0:T(8,128)}, u32[]{:S(2)}) copy-start(f32[512,512]{1,0:T(8,128)} %param.17) | copy-start | bytes 3145732
  7.2 97.8 %copy-start.6 = (bf16[768,512]{1,0:T(8,128)(2,1)S(1)}, bf16[768,512]{1,0:T(8,128)(2,1)}, u32[]{:S(2)}) copy-start(bf16[768,512]{1,0:T(8,128)(2,1)} %param.15) | copy-start | bytes 2359300
  7.2 97.8 %all-gather.4.cloned.1.call-start = ((), (), s32[]{:S(2)}) async-start(), calls=%async_computation.1 | async-start | bytes 6684672 | tf_op jit(solution)/shard_map/all_gather | solution.py:30
  7.9 554.5 %reduce-scatter.2.cloned.1.call-start = ((), (), s32[]{:S(2)}) async-start(), calls=%async_computation.2 | async-start | bytes 17825792 | tf_op jit(solution)/shard_map/reduce_scatter | solution.py:67
  130.3 7.9 copy-start.2
  130.3 7.9 copy-start.4
  130.3 7.9 copy-start.5
  374.6 1.0 copy-start.1
  374.6 187.8 %copy-start.3 = (f32[512]{0:T(512)S(1)}, f32[512]{0:T(512)}, u32[]{:S(2)}) copy-start(f32[512]{0:T(512)} %param.16) | copy-start | bytes 6148
Sparse Core Ops, SparseCore 0:
  10.5 94.4 all-gather.3
  374.7 187.6 reduce-scatter.1
